TPU v7x, 32 devices: a whole 2x2x4 slice. The times are simulated.
32 devices in a mesh: groups: 2 (over x), hits: 8 (over z, y), heads: 2 (over core).
Axes of the slice: x: 2, y: 2, z: 4, core: 2. Of those that a mesh axis runs over, the one named last changes fastest.
Arguments:
- queries: bfloat16 [2048, 2048], P('groups', 'heads'), parts along dimension 0, may hold values from -13.5 to 13.5
- keys: bfloat16 [8192, 2048], P(('groups', 'hits'), 'heads'), parts along dimension 0, may hold values from -36 to 36
- values: bfloat16 [8192, 2048], P(('groups', 'hits'), 'heads'), parts along dimension 0, may hold values from -6 to 6
- hit_counts: int32 [16], P(('groups', 'hits')), parts along dimension 0, may hold values from 128 to 512, as said below
- latents: bfloat16 [2048, 2048], P(('groups', 'hits'), 'heads'), parts along dimension 0, may hold values from -23 to 23
- out_proj: bfloat16 [2048, 2048], P('heads'), may hold values from -1 to 1
- norm_gain: float32 [2048], P('heads'), may hold values from 0.1 to 1.9
- up_proj: bfloat16 [2048, 8192], P('heads', 'hits'), may hold values from -0.125 to 0.125
- down_proj: bfloat16 [8192, 2048], P('hits', 'heads'), may hold values from -0.25 to 0.25
Outputs:
- mixed: bfloat16 [2048, 2048], P(('groups', 'hits'), 'heads'), parts along dimension 0
There are 2 independent parts, one for each index of `groups`. A program takes and returns all parts, laid end to end along the dimension named above; an argument that names none is the same for every part. Nothing has to cross between parts.
Inputs may be any that keep to these rules, and one draw needn't show every extreme that they name: hit_counts[s] live hits fill the first slots of shard s; some shard is full and some holds exactly 128.
All inputs are finite; a program needn't handle non-finite values.
Results may differ from a plain program's by a relative error of at most 0.012.
Values may be sent and summed in bfloat16 or wider, within the bound.
No kernel may reach another device: no remote copies, remote signals or barrier semaphores. Data moves between devices by JAX's collectives and lax.ppermute only.
A program may use at most 64 MiB of HBM per device.

v0:
```python
import math
import jax
import jax.numpy as jnp
from jax import lax
from jax.sharding import PartitionSpec as P

D = 2048
HD = 128


def shards(queries, keys, values, hit_counts, latents, out_proj, norm_gain, up_proj, down_proj):
    width = keys.shape[1]
    local_heads = width // HD
    score_scale = 1.0 / math.sqrt(HD)
    live_mask = lax.broadcasted_iota(jnp.int32, (1, keys.shape[0]), 1) < hit_counts[0]

    def merged(row_top, row_total, context):
        row_best = lax.pmax(row_top, "hits")
        factor = jnp.exp(row_top - row_best)
        total_sum, context_sum = (
            lax.psum_scatter(row_total * factor, "hits", scatter_dimension=1, tiled=True),
            lax.psum_scatter(context * factor[..., None], "hits", scatter_dimension=1, tiled=True),
        )
        return (context_sum / total_sum[..., None]).astype(jnp.bfloat16)

    def one_head(head_index):
        col_start = head_index * HD
        q_head = lax.dynamic_slice_in_dim(queries, col_start, HD, 1)
        k_head = lax.dynamic_slice_in_dim(keys, col_start, HD, 1)
        v_head = lax.dynamic_slice_in_dim(values, col_start, HD, 1)
        scores = (
            lax.dot_general(
                q_head, k_head, (((1,), (1,)), ((), ())), preferred_element_type=jnp.float32
            )
            * score_scale
        )
        scores = jnp.where(live_mask, scores, -1e30)
        row_top = jnp.max(scores, axis=1)
        weights = jnp.where(live_mask, jnp.exp(scores - row_top[:, None]), 0.0)
        row_total = jnp.sum(weights, axis=1)
        context = jnp.dot(weights.astype(jnp.bfloat16), v_head, preferred_element_type=jnp.float32)
        return (row_top, row_total, context)

    context = merged(*lax.map(one_head, jnp.arange(local_heads, dtype=jnp.int32)))
    weights_out = out_proj.reshape(local_heads, HD, out_proj.shape[1])
    projected = jnp.einsum("hrd,hde->re", context, weights_out, preferred_element_type=jnp.float32)
    attended = lax.psum_scatter(projected, "heads", scatter_dimension=1, tiled=True)
    stream = latents.astype(jnp.float32) + attended
    squares = lax.psum(jnp.sum(stream * stream, axis=1), "heads")
    normed = (stream * lax.rsqrt(squares / D + 1e-06)[:, None] * norm_gain[None, :]).astype(
        jnp.bfloat16
    )
    partial_units = jnp.dot(
        lax.all_gather(normed, "hits", axis=0, tiled=True),
        up_proj,
        preferred_element_type=jnp.float32,
    )
    summed_units = lax.psum(partial_units, "heads")
    hidden = jax.nn.gelu(summed_units).astype(jnp.bfloat16)
    branch_out = lax.psum_scatter(
        jnp.dot(hidden, down_proj, preferred_element_type=jnp.float32),
        "hits",
        scatter_dimension=0,
        tiled=True,
    )
    return (stream + branch_out).astype(jnp.bfloat16)


def solution(mesh):
    return jax.shard_map(
        shards,
        mesh=mesh,
        in_specs=(
            P("groups", "heads"),
            P(("groups", "hits"), "heads"),
            P(("groups", "hits"), "heads"),
            P(("groups", "hits")),
            P(("groups", "hits"), "heads"),
            P("heads", None),
            P("heads"),
            P("heads", "hits"),
            P("hits", "heads"),
        ),
        out_specs=P(("groups", "hits"), "heads"),
        check_vma=False,
    )
```

profile of v0, /device:TPU:0, one launch (start us, length us, event | category | flops | bytes accessed | tf_op | source)
XLA Modules:
  0.0 451.4 jit_solution(14915383482989247984)
XLA Ops:
  6.5 54.9 %while.15 = (s32[]{:T(128)}, f32[8,1024]{1,0:T(8,128)S(1)}, f32[8,1024]{1,0:T(8,128)S(1)}, f32[8,1024,128]{2,1,0:T(8,128)}, s32[8]{0:T(128)S(1)}, /*index=5*/bf1...) while((s32[]{:T(128)}, f32[8,1024]{1,0:T(8,128)S(1)}, ...), condition=%wide.region_3.4_spmd.clone, body=%wide.region_0.3_spmd.clone.sunk | while | flops 275249664 | bytes 7376583 | solution.py:44
  6.6 0.7 dynamic_slice.34
  7.9 0.7 compare_reduce_fusion.2
  8.6 1.4 fusion.52
  10.1 2.5 fusion.54
  13.4 0.7 dynamic_slice.34
  14.8 0.7 compare_reduce_fusion.2
  15.4 1.4 fusion.52
  16.9 2.6 fusion.54
  20.3 0.7 dynamic_slice.34
  21.6 0.7 compare_reduce_fusion.2
  22.3 1.4 fusion.52
  23.8 2.6 fusion.54
  27.1 0.7 dynamic_slice.34
  28.5 0.7 compare_reduce_fusion.2
  29.2 1.4 fusion.52
  30.6 2.6 fusion.54
  34.0 0.7 dynamic_slice.34
  35.4 0.7 compare_reduce_fusion.2
  36.0 1.4 fusion.52
  37.5 2.6 fusion.54
  40.9 0.7 dynamic_slice.34
  42.2 0.7 compare_reduce_fusion.2
  42.9 1.4 fusion.52
  44.4 2.6 fusion.54
  47.7 0.7 dynamic_slice.34
  49.1 0.7 compare_reduce_fusion.2
  49.8 1.5 fusion.52
  51.2 2.5 fusion.54
  54.6 0.7 dynamic_slice.34
  56.0 0.7 compare_reduce_fusion.2
  56.6 1.4 fusion.52
  58.1 2.6 fusion.54
  61.5 38.9 %pmax.7 = f32[8,1024]{1,0:T(8,128)S(1)} all-reduce(f32[8,1024]{1,0:T(8,128)S(1)} %get-tuple-element.55), channel_id=1, replica_groups=mesh['groups'=2,'hits'=8,'heads'=2] {'hits'}, use_global_device_ids=true, to_apply=%region_4.5 | all-reduce | flops 8192 | bytes 65536 | tf_op jit(solution)/shard_map/pmax | solution.py:18
  101.0 4.2 broadcast_multiply_fusion
  105.3 47.9 %reduce-scatter.7.cloned.1.call-done = f32[8,128]{1,0:T(8,128)} async-done(((f32[8,1024]{1,0:T(8,128)}), f32[8,128]{1,0:T(8,128)}) %reduce-scatter.7.cloned.1.call-update) | async-done | bytes 4112 | tf_op jit(solution)/shard_map/reduce_scatter | solution.py:21
  153.2 91.0 %reduce-scatter.5.cloned.1.call-done = f32[8,128,128]{2,1,0:T(8,128)} async-done(((f32[8,1024,128]{2,1,0:T(8,128)}), f32[8,128,128]{2,1,0:T(8,128)}) %reduce-scatter.5.cloned.1.call-update) | async-done | bytes 524304 | tf_op jit(solution)/shard_map/reduce_scatter | solution.py:22
  244.2 4.2 convolution_bitcast_fusion.1
  248.4 8.1 %reduce-scatter.9.cloned.1.call-done = f32[128,1024]{1,0:T(8,128)} async-done(((f32[128,2048]{1,0:T(8,128)}), f32[128,1024]{1,0:T(8,128)}) %reduce-scatter.9.cloned.1.call-update) | async-done | bytes 524304 | tf_op jit(solution)/shard_map/reduce_scatter | solution.py:47
  256.5 1.2 multiply_reduce_fusion
  257.7 2.5 psum.14
  260.2 1.9 multiply_convert_fusion
  262.1 50.4 %all-gather.2.cloned.1.call-done = bf16[1024,1024]{1,0:T(8,128)(2,1)} async-done(((bf16[128,1024]{1,0:T(8,128)(2,1)}), bf16[1024,1024]{1,0:T(8,128)(2,1)}) %all-gather.2.cloned.1.call-update) | async-done | bytes 2097168 | tf_op jit(solution)/shard_map/all_gather | solution.py:54
  312.5 5.9 %fusion.40 = f32[1024,1024]{1,0:T(8,128)} fusion(bf16[1024,1024]{1,0:T(8,128)(2,1)} %all-gather.2.cloned.1.call-done, bf16[1024,1024]{1,0:T(8,128)(2,1)S(1)} %copy-done), kind=kOutput, calls=%fused_computation.51 | convolution fusion | flops 2147483648 | bytes 8388608 | tf_op jit(solution)/shard_map/dot_general | solution.py:53
  318.5 26.7 %all-reduce.2.cloned.1.call-done = f32[1024,1024]{1,0:T(8,128)} async-done(((f32[1024,1024]{1,0:T(8,128)}), f32[1024,1024]{1,0:T(8,128)}) %all-reduce.2.cloned.1.call-update) | async-done | bytes 4194320 | tf_op jit(solution)/shard_map/psum | solution.py:58
  345.2 7.5 %fusion.28 = f32[1024,1024]{1,0:T(8,128)} fusion(bf16[1024,1024]{1,0:T(8,128)(2,1)} %param.19, f32[1024,1024]{1,0:T(8,128)} %all-reduce.2.cloned.1.call-done), kind=kOutput, calls=%fused_computation.32 | convolution fusion | flops 2156920832 | bytes 10485760 | tf_op jit(solution)/shard_map/dot_general | solution.py:61
  352.7 90.0 %reduce-scatter.11.cloned.1.call-done = f32[128,1024]{1,0:T(8,128)} async-done(((f32[1024,1024]{1,0:T(8,128)}), f32[128,1024]{1,0:T(8,128)}) %reduce-scatter.11.cloned.1.call-update) | async-done | bytes 524304 | tf_op jit(solution)/shard_map/reduce_scatter | solution.py:60
  442.8 1.8 add_convert_fusion
  (50 shorter events, 7.2 us)
Async XLA Ops:
  6.5 306.0 %copy-start = (bf16[1024,1024]{1,0:T(8,128)(2,1)S(1)}, bf16[1024,1024]{1,0:T(8,128)(2,1)}, u32[]{:S(2)}) copy-start(bf16[1024,1024]{1,0:T(8,128)(2,1)} %param.18) | copy-start | bytes 6291460
  6.5 146.6 %reduce-scatter.7.cloned.1.call-start = ((), (), s32[]{:S(2)}) async-start(), calls=%async_computation.5 | async-start | bytes 36864 | tf_op jit(solution)/shard_map/reduce_scatter | solution.py:21
  101.0 143.2 %reduce-scatter.5.cloned.1.call-start = ((), (), s32[]{:S(2)}) async-start(), calls=%async_computation.4 | async-start | bytes 4718592 | tf_op jit(solution)/shard_map/reduce_scatter | solution.py:22
  105.3 151.3 %reduce-scatter.9.cloned.1.call-start = ((), (), s32[]{:S(2)}) async-start(), calls=%async_computation.6 | async-start | bytes 1572864 | tf_op jit(solution)/shard_map/reduce_scatter | solution.py:47
  244.2 12.4 %copy-start.2 = (bf16[128,1024]{1,0:T(8,128)(2,1)S(1)}, bf16[128,1024]{1,0:T(8,128)(2,1)}, u32[]{:S(2)}) copy-start(bf16[128,1024]{1,0:T(8,128)(2,1)} %param.15) | copy-start | bytes 786436
  244.2 16.0 %copy-start.3 = (f32[1024]{0:T(1024)S(1)}, f32[1024]{0:T(1024)}, u32[]{:S(2)}) copy-start(f32[1024]{0:T(1024)} %param.17) | copy-start | bytes 12292
  248.4 64.2 %all-gather.2.cloned.1.call-start = ((), (), s32[]{:S(2)}) async-start(), calls=%async_computation.7 | async-start | bytes 2359296 | tf_op jit(solution)/shard_map/all_gather | solution.py:54
  262.1 83.1 %all-reduce.2.cloned.1.call-start = ((), (), s32[]{:S(2)}) async-start(), calls=%async_computation.8 | async-start | bytes 8388608 | tf_op jit(solution)/shard_map/psum | solution.py:58
  318.5 124.3 %reduce-scatter.11.cloned.1.call-start = ((), (), s32[]{:S(2)}) async-start(), calls=%async_computation.9 | async-start | bytes 4718592 | tf_op jit(solution)/shard_map/reduce_scatter | solution.py:60
  352.7 90.1 %copy-start.1 = (f32[128,1024]{1,0:T(8,128)S(1)}, f32[128,1024]{1,0:T(8,128)}, u32[]{:S(2)}) copy-start(f32[128,1024]{1,0:T(8,128)} %reduce-scatter.9.cloned.1.call-done) | copy-start | bytes 1572868
Sparse Core Ops, SparseCore 0:
  101.1 52.0 reduce-scatter.6
  156.8 87.3 reduce-scatter.4
  248.5 8.0 reduce-scatter.8
  262.2 50.2 all-gather.1
  318.6 26.6 all-reduce.1
  352.9 89.8 reduce-scatter.10
where the time goes:
time: 452 us; the launch traced here: 451 us
  waiting for transfers between devices  314 us (69%)
  matrix products  49.5 us (11%)
  blocking collectives  41.3 us (9%)
  other arithmetic  19.6 us (4%)
  between operations  13.5 us (3%)
  local copies, waits for them, and re-layouts  7.08 us (2%)
  loops' own time  5.98 us (1%)
    reduce_scatter x1, waiting for transfers between devices, merged(): lax.psum_scatter(context * factor[..., None], 'hits', scatter_dimension=1...  91 us
    reduce_scatter x1, waiting for transfers between devices, shards(): lax.psum_scatter(jnp.dot(hidden, down_proj, preferred_element_type=jnp.fl...  90 us
    all_gather x1, waiting for transfers between devices, shards(): lax.all_gather(normed, 'hits', axis=0, tiled=True)  50.4 us
    reduce_scatter x1, waiting for transfers between devices, merged(): lax.psum_scatter(row_total * factor, 'hits', scatter_dimension=1, tiled=T...  47.9 us
    pmax x1, blocking collectives, merged(): row_best = lax.pmax(row_top, 'hits')  38.9 us
    psum x1, waiting for transfers between devices, shards(): summed_units = lax.psum(partial_units, 'heads')  26.7 us
    dot_general x8, matrix products, one_head(): jnp.dot(weights.astype(jnp.bfloat16), v_head, preferred_element_type=jnp....  20.5 us
    dot_general x8, matrix products, one_head(): lax.dot_general(q_head, k_head, (((1,), (1,)), ((), ())), preferred_eleme...  11.6 us
  transfers between devices with their start and end apart: 6, of which 6 were waited for; matrix products, arithmetic and copies ran while one was open for 1% of the time, Pallas kernels for 0%

commit v1 on v0

--- a/solution.py
+++ b/solution.py
@@ -6,6 +6,18 @@
 
 D = 2048
 HD = 128
+
+
+def gather_by_bits(x, axis, dim):
+    ways, here, step = (lax.axis_size(axis), lax.axis_index(axis), x.shape[dim])
+    line, have = (x, 1)
+    while have < ways:
+        line = jnp.concatenate(
+            [line, lax.ppermute(line, axis, [(d, (d - have) % ways) for d in range(ways)])],
+            axis=dim,
+        )
+        have = 2 * have
+    return jnp.roll(line, here * step, axis=dim)
 
 
 def shards(queries, keys, values, hit_counts, latents, out_proj, norm_gain, up_proj, down_proj):
@@ -51,9 +63,7 @@
         jnp.bfloat16
     )
     partial_units = jnp.dot(
-        lax.all_gather(normed, "hits", axis=0, tiled=True),
-        up_proj,
-        preferred_element_type=jnp.float32,
+        gather_by_bits(normed, "hits", 0), up_proj, preferred_element_type=jnp.float32
     )
     summed_units = lax.psum(partial_units, "heads")
     hidden = jax.nn.gelu(summed_units).astype(jnp.bfloat16)

time: 452 us -> 484 us (1.071)
  waiting for transfers between devices: 314 us -> 330 us
  local copies, waits for them, and re-layouts: 7.08 us -> 15.6 us
  starting transfers between devices: 0.21 us -> 7.04 us
    ppermute x0 -> x3, waiting for transfers between devices: none -> 62.7 us  [gather_by_bits(): lax.ppermute(line, axis, [(d, (d - have) % ways) for d in range(ways)])]
    all_gather x1 -> x0, waiting for transfers between devices: 50.4 us -> none  [shards(): lax.all_gather(normed, 'hits', axis=0, tiled=True)]
    ppermute x0 -> x3, starting transfers between devices: none -> 6.87 us  [gather_by_bits(): lax.ppermute(line, axis, [(d, (d - have) % ways) for d in range(ways)])]
    unnamed x8 -> x14, local copies, waits for them, and re-layouts: 0.02 us -> 6.22 us
  transfers between devices with their start and end apart: 6 -> 8, of which waited for: 6 -> 8; matrix products, arithmetic and copies ran while one was open for 1% -> 1% of each run, Pallas kernels for 0% -> 0%
where the time goes in v1:
time: 484 us; the launch traced here: 483 us
  waiting for transfers between devices  330 us (68%)
  matrix products  49.5 us (10%)
  blocking collectives  41.3 us (9%)
  other arithmetic  20.7 us (4%)
  local copies, waits for them, and re-layouts  15.6 us (3%)
  between operations  13.2 us (3%)
  starting transfers between devices  7.04 us (1%)
  loops' own time  5.98 us (1%)
    reduce_scatter x1, waiting for transfers between devices, merged(): lax.psum_scatter(context * factor[..., None], 'hits', scatter_dimension=1...  91 us
    reduce_scatter x1, waiting for transfers between devices, shards(): lax.psum_scatter(jnp.dot(hidden, down_proj, preferred_element_type=jnp.fl...  90.1 us
    ppermute x3, waiting for transfers between devices, gather_by_bits(): lax.ppermute(line, axis, [(d, (d - have) % ways) for d in range(ways)])  62.7 us
    reduce_scatter x1, waiting for transfers between devices, merged(): lax.psum_scatter(row_total * factor, 'hits', scatter_dimension=1, tiled=T...  47.8 us
    pmax x1, blocking collectives, merged(): row_best = lax.pmax(row_top, 'hits')  38.9 us
    psum x1, waiting for transfers between devices, shards(): summed_units = lax.psum(partial_units, 'heads')  30.1 us
    dot_general x8, matrix products, one_head(): jnp.dot(weights.astype(jnp.bfloat16), v_head, preferred_element_type=jnp....  20.5 us
    dot_general x8, matrix products, one_head(): lax.dot_general(q_head, k_head, (((1,), (1,)), ((), ())), preferred_eleme...  11.6 us
  transfers between devices with their start and end apart: 8, of which 8 were waited for; matrix products, arithmetic and copies ran while one was open for 1% of the time, Pallas kernels for 0%

profile of v1, /device:TPU:0, one launch (start us, length us, event | category | flops | bytes accessed | tf_op | source)
XLA Modules:
  0.0 483.2 jit_solution(7576463780497924961)
XLA Ops:
  6.5 54.9 %while.15 = (s32[]{:T(128)}, f32[8,1024]{1,0:T(8,128)S(1)}, f32[8,1024]{1,0:T(8,128)S(1)}, f32[8,1024,128]{2,1,0:T(8,128)}, s32[8]{0:T(128)S(1)}, /*index=5*/bf1...) while((s32[]{:T(128)}, f32[8,1024]{1,0:T(8,128)S(1)}, ...), condition=%wide.region_3.4_spmd.clone, body=%wide.region_0.3_spmd.clone.sunk | while | flops 275249664 | bytes 7376583 | solution.py:56
  7.9 0.7 compare_reduce_fusion.2
  8.6 1.4 fusion.53
  10.1 2.5 fusion.55
  14.8 0.7 compare_reduce_fusion.2
  15.4 1.4 fusion.53
  16.9 2.6 fusion.55
  21.6 0.7 compare_reduce_fusion.2
  22.3 1.4 fusion.53
  23.8 2.6 fusion.55
  29.2 1.4 fusion.53
  30.6 2.6 fusion.55
  36.0 1.4 fusion.53
  37.5 2.6 fusion.55
  42.9 1.4 fusion.53
  44.4 2.6 fusion.55
  49.8 1.5 fusion.53
  51.2 2.5 fusion.55
  56.6 1.4 fusion.53
  58.1 2.6 fusion.55
  61.5 38.9 %pmax.7 = f32[8,1024]{1,0:T(8,128)S(1)} all-reduce(f32[8,1024]{1,0:T(8,128)S(1)} %get-tuple-element.55), channel_id=1, replica_groups=mesh['groups'=2,'hits'=8,'heads'=2] {'hits'}, use_global_device_ids=true, to_apply=%region_4.5 | all-reduce | flops 8192 | bytes 65536 | tf_op jit(solution)/shard_map/pmax | solution.py:30
  101.0 4.2 broadcast_multiply_fusion
  105.3 47.8 %reduce-scatter.7.cloned.1.call-done = f32[8,128]{1,0:T(8,128)} async-done(((f32[8,1024]{1,0:T(8,128)}), f32[8,128]{1,0:T(8,128)}) %reduce-scatter.7.cloned.1.call-update) | async-done | bytes 4112 | tf_op jit(solution)/shard_map/reduce_scatter | solution.py:33
  153.2 91.0 %reduce-scatter.5.cloned.1.call-done = f32[8,128,128]{2,1,0:T(8,128)} async-done(((f32[8,1024,128]{2,1,0:T(8,128)}), f32[8,128,128]{2,1,0:T(8,128)}) %reduce-scatter.5.cloned.1.call-update) | async-done | bytes 524304 | tf_op jit(solution)/shard_map/reduce_scatter | solution.py:34
  244.2 4.1 convolution_bitcast_fusion.1
  248.4 8.1 %reduce-scatter.9.cloned.1.call-done = f32[128,1024]{1,0:T(8,128)} async-done(((f32[128,2048]{1,0:T(8,128)}), f32[128,1024]{1,0:T(8,128)}) %reduce-scatter.9.cloned.1.call-update) | async-done | bytes 524304 | tf_op jit(solution)/shard_map/reduce_scatter | solution.py:59
  256.5 1.2 multiply_reduce_fusion
  257.7 2.5 psum.14
  260.2 1.9 constant_dynamic-update-slice_fusion.7
  262.0 4.5 collective-permute-start
  266.6 6.0 %collective-permute-done = bf16[128,1024]{1,0:T(8,128)(2,1)S(1)} collective-permute-done((bf16[128,1024]{1,0:T(8,128)(2,1)S(1)}, bf16[128,1024]{1,0:T(8,128)(2,1)S(1)}, u32[]{:S(2)}, u32[]{:S(2)}) %collective-permute-start) | collective-permute-done | bytes 262176 | tf_op jit(solution)/shard_map/ppermute | solution.py:16
  272.6 1.6 collective-permute-start.1
  274.2 11.7 %collective-permute-done.1 = bf16[256,1024]{1,0:T(8,128)(2,1)S(1)} collective-permute-done((bf16[256,1024]{1,0:T(8,128)(2,1)S(1)}, bf16[256,1024]{1,0:T(8,128)(2,1)S(1)}, u32[]{:S(2)}, u32[]{:S(2)}) %collective-permute-start.1) | collective-permute-done | bytes 524320 | tf_op jit(solution)/shard_map/ppermute | solution.py:16
  285.9 1.1 pad_maximum_fusion
  287.0 0.7 collective-permute-start.2
  287.7 0.7 constant_dynamic-update-slice_fusion.6
  288.4 0.8 constant_dynamic-update-slice_fusion.5
  289.2 45.0 %collective-permute-done.2 = bf16[512,1024]{1,0:T(8,128)(2,1)} collective-permute-done((bf16[512,1024]{1,0:T(8,128)(2,1)}, bf16[512,1024]{1,0:T(8,128)(2,1)}, u32[]{:S(2)}, u32[]{:S(2)}) %collective-permute-start.2) | collective-permute-done | bytes 1048608 | tf_op jit(solution)/shard_map/ppermute | solution.py:16
  334.3 2.3 constant_dynamic-update-slice_fusion.4
  336.6 0.7 constant_dynamic-update-slice_fusion.3
  337.3 0.7 constant_dynamic-update-slice_fusion.2
  338.1 0.8 constant_dynamic-update-slice_fusion.1
  338.9 2.3 constant_dynamic-update-slice_fusion
  341.2 5.9 %fusion.34 = f32[1024,1024]{1,0:T(8,128)} fusion(bf16[1024,1024]{1,0:T(8,128)(2,1)S(1)} %copy-done, bf16[2048,1024]{1,0:T(8,128)(2,1)} %constant_dynamic-update-slice_fusion, s32[]{:T(128)S(6)} %select_n.26), kind=kOutput, calls=%fused_computation.37 | convolution fusion | flops 2147483648 | bytes 8388612 | tf_op jit(solution)/shard_map/dot_general | solution.py:65
  347.1 30.1 %all-reduce.2.cloned.1.call-done = f32[1024,1024]{1,0:T(8,128)} async-done(((f32[1024,1024]{1,0:T(8,128)}), f32[1024,1024]{1,0:T(8,128)}) %all-reduce.2.cloned.1.call-update) | async-done | bytes 4194320 | tf_op jit(solution)/shard_map/psum | solution.py:68
  377.2 7.5 %fusion.28 = f32[1024,1024]{1,0:T(8,128)} fusion(bf16[1024,1024]{1,0:T(8,128)(2,1)} %param.19, f32[1024,1024]{1,0:T(8,128)} %all-reduce.2.cloned.1.call-done), kind=kOutput, calls=%fused_computation.32 | convolution fusion | flops 2156920832 | bytes 10485760 | tf_op jit(solution)/shard_map/dot_general | solution.py:71
  384.7 90.1 %reduce-scatter.11.cloned.1.call-done = f32[128,1024]{1,0:T(8,128)} async-done(((f32[1024,1024]{1,0:T(8,128)}), f32[128,1024]{1,0:T(8,128)}) %reduce-scatter.11.cloned.1.call-update) | async-done | bytes 524304 | tf_op jit(solution)/shard_map/reduce_scatter | solution.py:70
  474.8 1.8 add_convert_fusion
  (62 shorter events, 15.8 us)
Async XLA Ops:
  6.5 334.6 %copy-start = (bf16[1024,1024]{1,0:T(8,128)(2,1)S(1)}, bf16[1024,1024]{1,0:T(8,128)(2,1)}, u32[]{:S(2)}) copy-start(bf16[1024,1024]{1,0:T(8,128)(2,1)} %param.18) | copy-start | bytes 6291460
  6.5 146.6 %reduce-scatter.7.cloned.1.call-start = ((), (), s32[]{:S(2)}) async-start(), calls=%async_computation.5 | async-start | bytes 36864 | tf_op jit(solution)/shard_map/reduce_scatter | solution.py:33
  101.0 143.2 %reduce-scatter.5.cloned.1.call-start = ((), (), s32[]{:S(2)}) async-start(), calls=%async_computation.4 | async-start | bytes 4718592 | tf_op jit(solution)/shard_map/reduce_scatter | solution.py:34
  105.3 151.3 %copy-start.2 = (bf16[128,1024]{1,0:T(8,128)(2,1)S(1)}, bf16[128,1024]{1,0:T(8,128)(2,1)}, u32[]{:S(2)}) copy-start(bf16[128,1024]{1,0:T(8,128)(2,1)} %param.15) | copy-start | bytes 786436
  105.3 154.9 %copy-start.3 = (f32[1024]{0:T(1024)S(1)}, f32[1024]{0:T(1024)}, u32[]{:S(2)}) copy-start(f32[1024]{0:T(1024)} %param.17) | copy-start | bytes 12292
  105.3 151.2 %reduce-scatter.9.cloned.1.call-start = ((), (), s32[]{:S(2)}) async-start(), calls=%async_computation.6 | async-start | bytes 1572864 | tf_op jit(solution)/shard_map/reduce_scatter | solution.py:59
  248.3 128.9 %all-reduce.2.cloned.1.call-start = ((), (), s32[]{:S(2)}) async-start(), calls=%async_computation.7 | async-start | bytes 8388608 | tf_op jit(solution)/shard_map/psum | solution.py:68
  262.0 10.5 %collective-permute-start = (bf16[128,1024]{1,0:T(8,128)(2,1)S(1)}, bf16[128,1024]{1,0:T(8,128)(2,1)S(1)}, u32[]{:S(2)}, u32[]{:S(2)}) collective-permute-start(bf16[128,1024]{1,0:T(8,128)(2,1)S(1)} %get-tuple-element.97), channel_id=1, source_target_pairs={{0,14},{2,0},{4,2},{6,4},{8,6},{10,8},{12,10},{14,12},{1,15},{3,1}... | collective-permute-start | bytes 786440 | tf_op jit(solution)/shard_map/ppermute | solution.py:16
  272.6 13.3 %collective-permute-start.1 = (bf16[256,1024]{1,0:T(8,128)(2,1)S(1)}, bf16[256,1024]{1,0:T(8,128)(2,1)S(1)}, u32[]{:S(2)}, u32[]{:S(2)}) collective-permute-start(bf16[256,1024]{1,0:T(8,128)(2,1)S(1)} %pad_maximum_fusion.1), channel_id=1, source_target_pairs={{0,12},{2,14},{4,0},{6,2},{8,4},{10,6},{12,8},{14,10},{1,13},{3,15... | collective-permute-start | bytes 1572872 | tf_op jit(solution)/shard_map/ppermute | solution.py:16
  287.0 47.3 %collective-permute-start.2 = (bf16[512,1024]{1,0:T(8,128)(2,1)}, bf16[512,1024]{1,0:T(8,128)(2,1)}, u32[]{:S(2)}, u32[]{:S(2)}) collective-permute-start(bf16[512,1024]{1,0:T(8,128)(2,1)} %pad_maximum_fusion), channel_id=1, source_target_pairs={{0,8},{2,10},{4,12},{6,14},{8,0},{10,2},{12,4},{14,6},{1,9},{3,11}... | collective-permute-start | bytes 3145736 | tf_op jit(solution)/shard_map/ppermute | solution.py:16
  347.1 127.7 %reduce-scatter.11.cloned.1.call-start = ((), (), s32[]{:S(2)}) async-start(), calls=%async_computation.8 | async-start | bytes 4718592 | tf_op jit(solution)/shard_map/reduce_scatter | solution.py:70
  384.7 90.1 %copy-start.1 = (f32[128,1024]{1,0:T(8,128)S(1)}, f32[128,1024]{1,0:T(8,128)}, u32[]{:S(2)}) copy-start(f32[128,1024]{1,0:T(8,128)} %reduce-scatter.9.cloned.1.call-done) | copy-start | bytes 1572868
Sparse Core Ops, SparseCore 0:
  101.1 52.0 reduce-scatter.6
  156.8 87.3 reduce-scatter.4
  248.4 8.0 reduce-scatter.8
  347.2 29.9 all-reduce.1
  384.8 89.9 reduce-scatter.10
